TPU v7x, 512 devices: a whole 4x8x8 slice. The times are simulated.
512 devices in a mesh: head: 8 (over z), blk: 64 (over x, y, core).
Axes of the slice: x: 4, y: 8, z: 8, core: 2. Of those that a mesh axis runs over, the one named last changes fastest.
Arguments:
- vision: bfloat16 [4, 1408, 8192], P(None, 'head', 'blk'), may hold values from -600 to 600
- ln_gain: float32 [1408], P('head'), may hold values from 0.5 to 1.5
- merge_proj: bfloat16 [4, 1408, 1408], P(None, 'head'), may hold values from -0.078125 to 0.078125
- image_slot: int32 [2048], P('blk'), may hold values from 0 to 32764, as said below
- text: bfloat16 [1408, 32768], P('head', 'blk'), may hold values from -600 to 600
- rms_gain: float32 [1408], replicated, may hold values from 0.5 to 1.5
- wqkv: bfloat16 [3, 1408, 1408], P(None, 'head'), may hold values from -0.31835938 to 0.31835938
- pcache: bfloat16 [2, 1408, 131072], P(None, 'head', 'blk'), may hold values from -300 to 300
- block_table: int32 [64, 128], replicated, may hold values from -1 to 4095, as said below
- cache_len: int32 [64], P('blk'), may hold values from 1 to 4096, as said below
Outputs:
- attended: bfloat16 [1408, 32768], P('head', 'blk')
- new_cache: bfloat16 [2, 1408, 32768], P(None, 'head', 'blk')
Inputs may be any that keep to these rules, and one draw needn't show every extreme that they name: `image_slot`: pieces never intersect and start at multiples of 4; the 32 pieces held by one index of blk start in the rows of 32 different requests, and every request receives exactly 32 pieces. `block_table`: row r holds a block number for j < ceil(cache_len[r] / 32) and -1 after; no block number appears twice; index d of blk holds blocks d * 64 to (d+1) * 64 - 1. The longest request has exactly 2 blocks on every index of blk; every other request has at most one block on any index. `cache_len`: exactly one request, the longest, has 4096 cached positions; all others have fewer.
All inputs are finite; a program needn't handle non-finite values.
Results may differ from a plain program's by a relative error of at most 0.025.
The roundings to bfloat16 on the way count: a program that leaves them out, or rounds other values in their place, can miss the bound.
Values may be sent and summed in bfloat16 or wider, within the bound.
A program may use at most 128 MiB of HBM per device.

v0:
```python
import math
import jax
import jax.numpy as jnp
from jax import lax
from jax.sharding import PartitionSpec as P

D = 1408
HD = 88
BS = 32
masked_score = -1e30


def rotary_columns(values, places):
    half = values.shape[1] // 2
    freq_index = jnp.arange(half, dtype=jnp.float32)
    inverse = jnp.exp(freq_index * (-2.0 * math.log(10000.0) / values.shape[1]))
    angles = inverse[:, None] * places[None, :]
    cosine = jnp.cos(angles)[None]
    sine_part = jnp.sin(angles)[None]
    leading = values[:, :half]
    trailing = values[:, half:]
    return jnp.concatenate(
        [leading * cosine - trailing * sine_part, trailing * cosine + leading * sine_part], axis=1
    )


def softmax_part(query_block, keys, values, mask, scale):
    scores = (
        jnp.einsum("hdq,hdk->hqk", query_block, keys, preferred_element_type=jnp.float32) * scale
    )
    scores = jnp.where(mask[None], scores, masked_score)
    highest = jnp.max(scores, axis=2)
    expo = jnp.where(mask[None], jnp.exp(scores - highest[:, :, None]), 0.0)
    total = jnp.sum(expo, axis=2)
    mixed = jnp.einsum("hqk,hdk->hdq", expo, values, precision=lax.Precision.HIGHEST)
    return (mixed, highest, total)


def fold_softmax(first, second):
    mixed_a, high_a, total_a = first
    mixed_b, high_b, total_b = second
    top = jnp.maximum(high_a, high_b)
    factor_a = jnp.exp(high_a - top)
    factor_b = jnp.exp(high_b - top)
    return (
        mixed_a * factor_a[:, None, :] + mixed_b * factor_b[:, None, :],
        top,
        total_a * factor_a + total_b * factor_b,
    )


def unblock(parts):
    mixed, highest, total = parts
    heads_here = mixed.shape[1]
    mixed = jnp.transpose(mixed, (1, 2, 0, 3)).reshape(heads_here, mixed.shape[2], -1)
    highest = jnp.transpose(highest, (1, 0, 2)).reshape(heads_here, -1)
    total = jnp.transpose(total, (1, 0, 2)).reshape(heads_here, -1)
    return (mixed, highest, total)


def shards(
    vision, ln_gain, merge_proj, image_slot, text, rms_gain, wqkv, pcache, block_table, cache_len
):
    local = vision.shape[1]
    groups = vision.shape[2]
    floats = vision.astype(jnp.float32)
    totals, squares = lax.psum((jnp.sum(floats, axis=1), jnp.sum(floats * floats, axis=1)), "head")
    average = totals / D
    spread = squares / D - average * average
    normed_vision = (
        (floats - average[:, None, :])
        * lax.rsqrt(spread + 1e-06)[:, None, :]
        * ln_gain[None, :, None]
    ).astype(jnp.bfloat16)
    partial_rows = jnp.einsum(
        "tcd,tcg->dg", merge_proj, normed_vision, preferred_element_type=jnp.float32
    )
    merged_columns = lax.psum_scatter(partial_rows, "head", scatter_dimension=0, tiled=True).astype(
        jnp.bfloat16
    )
    merged = jnp.transpose(merged_columns)
    devices = lax.axis_size("blk")
    here = lax.axis_index("blk")
    rows_here = text.shape[1]
    pieces = image_slot.shape[0]
    piece_rows = groups // pieces
    lines = jnp.arange(rows_here, dtype=jnp.int32)
    offsets = jnp.arange(piece_rows, dtype=jnp.int32)
    target = image_slot // rows_here
    within = image_slot % rows_here
    select = target[None, :] == jnp.arange(devices, dtype=jnp.int32)[:, None]
    outbound = (
        jnp.dot(
            select.astype(jnp.bfloat16),
            merged.reshape(pieces, piece_rows * local),
            preferred_element_type=jnp.float32,
        )
        .astype(jnp.bfloat16)
        .reshape(devices, piece_rows, local)
    )
    starts = jnp.sum(jnp.where(select, within[None, :] + 1, 0), axis=1) - 1
    arrived, arrived_start = (
        lax.all_to_all(outbound, "blk", split_axis=0, concat_axis=0, tiled=True),
        lax.all_to_all(starts, "blk", split_axis=0, concat_axis=0, tiled=True),
    )
    row_ids = (arrived_start[:, None] + offsets[None, :]).reshape(-1)
    present = jnp.repeat(arrived_start >= 0, piece_rows)
    hits = (row_ids[:, None] == lines[None, :]) & present[:, None]
    placed_rows = jnp.einsum(
        "kl,kr->lr",
        arrived.reshape(devices * piece_rows, local),
        hits.astype(jnp.bfloat16),
        preferred_element_type=jnp.float32,
    ).astype(jnp.bfloat16)
    covered = jnp.any(hits, axis=0)
    placed = jnp.where(covered[None, :], placed_rows, text)
    row_floats = placed.astype(jnp.float32)
    square_sums = lax.psum(jnp.sum(row_floats * row_floats, axis=0), "head")
    gain_here = lax.dynamic_slice_in_dim(rms_gain, lax.axis_index("head") * local, local)
    normed = (row_floats * lax.rsqrt(square_sums / D + 1e-06)[None, :] * gain_here[:, None]).astype(
        jnp.bfloat16
    )
    projected = jnp.einsum(
        "jod,dr->jor",
        wqkv,
        lax.all_gather(normed, "head", axis=0, tiled=True),
        preferred_element_type=jnp.float32,
    )
    heads_here = local // HD
    projected = projected.reshape(3, heads_here, HD, rows_here)
    places = (cache_len[0] + lines).astype(jnp.float32)
    queries = rotary_columns(projected[0], places).astype(jnp.bfloat16)
    new_keys = rotary_columns(projected[1], places).astype(jnp.bfloat16)
    new_values = projected[2].astype(jnp.bfloat16)
    new_cache = jnp.stack(
        [new_keys.reshape(local, rows_here), new_values.reshape(local, rows_here)], axis=0
    )
    block_len = BS
    owned = pcache.shape[2] // block_len
    paged = pcache.reshape(2, local, owned, block_len)
    requests = block_table.shape[0]
    table_width = block_table.shape[1]
    slots_each = table_width // devices
    block_ids = here * owned + jnp.arange(owned, dtype=jnp.int32)
    matches = block_table[None, :, :] == block_ids[:, None, None]
    found = jnp.any(matches, axis=2)
    in_use = jnp.any(found, axis=1)
    owner = jnp.sum(jnp.where(found, jnp.arange(requests, dtype=jnp.int32)[None, :], 0), axis=1)
    logical = jnp.sum(
        jnp.where(matches, jnp.arange(table_width, dtype=jnp.int32)[None, None, :], 0), axis=(1, 2)
    )
    counter = jnp.arange(owned, dtype=jnp.int32)
    earlier = (
        (owner[:, None] == owner[None, :]) & in_use[None, :] & (counter[None, :] < counter[:, None])
    )
    standing = jnp.sum(earlier.astype(jnp.int32), axis=1)
    within_block = jnp.arange(block_len, dtype=jnp.int32)
    block_rows = min(rows_here, 512)
    count_blocks = rows_here // block_rows
    scale = HD ** (-0.5)
    query_blocks = jnp.transpose(
        queries.reshape(heads_here, HD, count_blocks, block_rows), (2, 0, 1, 3)
    )
    first_rows = jnp.arange(count_blocks, dtype=jnp.int32) * block_rows
    destination = owner * slots_each + standing
    routing = (destination[None, :] == jnp.arange(table_width, dtype=jnp.int32)[:, None]) & in_use[
        None, :
    ]
    outgoing = jnp.einsum(
        "wo,cfob->cfwb", routing.astype(jnp.bfloat16), paged, preferred_element_type=jnp.float32
    ).astype(jnp.bfloat16)
    outgoing = outgoing.reshape(2, local, table_width * block_len)
    labels = jnp.sum(jnp.where(routing, logical[None, :] + 1, 0), axis=1) - 1
    labels = labels.reshape(1, 1, table_width)
    blocks_in, labels_in = (
        lax.all_to_all(outgoing, "blk", split_axis=2, concat_axis=2, tiled=True),
        lax.all_to_all(labels, "blk", split_axis=2, concat_axis=2, tiled=True),
    )
    cached_keys = blocks_in[0].reshape(heads_here, HD, -1)
    cached_values = blocks_in[1].reshape(heads_here, HD, -1).astype(jnp.float32)
    label_flat = labels_in.reshape(-1)
    key_places = label_flat[:, None] * block_len + within_block[None, :]
    live = ((label_flat[:, None] >= 0) & (key_places < cache_len[0])).reshape(-1)
    old_mask = jnp.broadcast_to(live[None, :], (block_rows, live.shape[0]))
    new_values_f = new_values.astype(jnp.float32)

    def attend(inputs):
        query_block, first_row = inputs
        causal = (first_row + jnp.arange(block_rows, dtype=jnp.int32))[:, None] >= lines[None, :]
        old_part = softmax_part(query_block, cached_keys, cached_values, old_mask, scale)
        own_part = softmax_part(query_block, new_keys, new_values_f, causal, scale)
        return fold_softmax(old_part, own_part)

    mixed, highest, total = unblock(lax.map(attend, (query_blocks, first_rows)))
    attended = (mixed / total[:, None, :]).astype(jnp.bfloat16).reshape(local, rows_here)
    return (attended, new_cache)


def solution(mesh):
    in_specs = (
        P(None, "head", "blk"),
        P("head"),
        P(None, "head", None),
        P("blk"),
        P("head", "blk"),
        P(),
        P(None, "head", None),
        P(None, "head", "blk"),
        P(),
        P("blk"),
    )
    out_specs = (P("head", "blk"), P(None, "head", "blk"))
    return jax.shard_map(shards, mesh=mesh, in_specs=in_specs, out_specs=out_specs, check_vma=False)
```

profile of v0, /device:TPU:1, one launch (start us, length us, event | category | flops | bytes accessed | tf_op | source)
XLA Modules:
  0.0 288.2 jit_solution(1287686254156349032)
XLA Ops:
  8.3 20.3 %all-reduce = (f32[4,128]{1,0:T(4,128)S(1)}, f32[4,128]{1,0:T(4,128)S(1)}) all-reduce(f32[4,128]{1,0:T(4,128)S(1)} %get-tuple-element.23, f32[4,128]{1,0:T(4,128)S(1)} %get-tuple-element.22), channel_id=1, replica_groups=mesh['head'=8,'blk'=64] {'head'}, use_global_device_ids=true, to_apply=%region_11.12 | all-reduce | flops 1024 | bytes 8192 | tf_op jit(solution)/shard_map/psum | solution.py:67
  32.2 14.5 %all-to-all-start.2 = ((s32[64,1,1]{2,1,0:T(1,128)}), s32[64,1,1]{2,1,0:T(1,128)S(1)}, u32[]{:S(2)}, u32[]{:S(2)}) async-start(s32[64,1,1]{2,1,0:T(1,128)} %copy.44), calls=%async_computation.2 | async-start | bytes 65536 | tf_op jit(solution)/shard_map/all_to_all | solution.py:104
  46.8 2.4 compare_reduce_fusion
  51.7 3.7 %copy.38 = bf16[2,176,2048]{1,2,0:T(8,128)(2,1)} copy(bf16[2,176,2048]{2,1,0:T(8,128)(2,1)} %param.17) | data formatting | bytes 2883584 | tf_op args[7]
  55.4 13.9 %reduce-scatter.4.cloned.1.call-done = f32[176,128]{1,0:T(8,128)} async-done(((f32[1408,128]{1,0:T(8,128)}), f32[176,128]{1,0:T(8,128)}) %reduce-scatter.4.cloned.1.call-update) | async-done | bytes 90128
  70.4 14.6 %all-to-all-start.1 = ((s32[1,1,128]{1,0,2:T(1,128)}), s32[1,1,128]{1,0,2:T(1,128)S(1)}, u32[]{:S(2)}, u32[]{:S(2)}) async-start(s32[1,1,128]{1,0,2:T(1,128)} %copy.43), calls=%async_computation.1 | async-start | bytes 131072 | tf_op jit(solution)/shard_map/all_to_all | solution.py:177
  86.1 8.7 %all-to-all-done.1 = s32[1,1,128]{1,0,2:T(1,128)S(1)} async-done(((s32[1,1,128]{1,0,2:T(1,128)}), s32[1,1,128]{1,0,2:T(1,128)S(1)}, u32[]{:S(2)}, u32[]{:S(2)}) %all-to-all-start.1) | async-done | bytes 544 | tf_op jit(solution)/shard_map/all_to_all | solution.py:177
  94.8 4.4 %all-to-all-start.3 = ((bf16[64,4,176]{2,1,0:T(4,128)(2,1)}), bf16[64,4,176]{2,1,0:T(4,128)(2,1)S(1)}, u32[]{:S(2)}, u32[]{:S(2)}) async-start(bf16[64,4,176]{2,1,0:T(4,128)(2,1)} %reshape.266), calls=%async_computation.3 | async-start | bytes 262144 | tf_op jit(solution)/shard_map/all_to_all | solution.py:103
  99.2 4.9 %convert_bitcast_fusion = bf16[2,176,128,32]{2,1,3,0:T(8,128)(2,1)} fusion(bf16[2,176,64,32]{1,3,2,0:T(8,128)(2,1)} %bitcast.47, s32[64]{0:T(128)S(1)} %get-tuple-element.61, pred[64]{0:T(512)(128)(4,1)S(1)} %get-tuple-element.24), kind=kOutput, calls=%fused_computation.13 | convolution fusion | flops 186007552 | bytes 4325696 | tf_op jit(solution)/shard_map/wo,cfob->cfwb/dot_general | solution.py:169
  104.1 7.7 %copy.40 = bf16[2,176,128,32]{1,3,2,0:T(8,128)(2,1)} copy(bf16[2,176,128,32]{2,1,3,0:T(8,128)(2,1)} %convert_bitcast_fusion) | data formatting | bytes 5767168 | tf_op jit(solution)/shard_map/convert_element_type | solution.py:171
  111.8 10.1 %copy.41 = bf16[2,176,4096]{1,0,2:T(2,128)(2,1)} copy(bf16[2,176,4096]{1,2,0:T(8,128)(2,1)} %bitcast.46) | data formatting | bytes 5767168 | tf_op jit(solution)/shard_map/reshape | solution.py:172
  121.9 10.8 %all-to-all-start = ((bf16[2,176,4096]{1,0,2:T(2,128)(2,1)}), bf16[2,176,4096]{1,0,2:T(2,128)(2,1)}, u32[]{:S(2)}, u32[]{:S(2)}) async-start(bf16[2,176,4096]{1,0,2:T(2,128)(2,1)} %copy.41), calls=%async_computation | async-start | bytes 8388608 | tf_op jit(solution)/shard_map/all_to_all | solution.py:176
  135.7 13.1 %psum.23 = f32[512]{0:T(512)S(1)} all-reduce(f32[512]{0:T(512)S(1)} %get-tuple-element.55), channel_id=1, replica_groups=mesh['head'=8,'blk'=64] {'head'}, use_global_device_ids=true, to_apply=%region_14.15 | all-reduce | flops 512 | bytes 4096 | tf_op jit(solution)/shard_map/psum | solution.py:118
  150.9 2.4 multiply_reduce_fusion.1
  153.2 2.4 compare_reduce_fusion.2
  155.8 34.9 %all-gather.2.cloned.1.call-done = bf16[1408,512]{1,0:T(8,128)(2,1)} async-done(((bf16[176,512]{1,0:T(8,128)(2,1)}), bf16[1408,512]{1,0:T(8,128)(2,1)}) %all-gather.2.cloned.1.call-update) | async-done | bytes 1441808 | tf_op jit(solution)/shard_map/all_gather | solution.py:126
  190.7 2.8 fusion.15
  197.2 31.4 %all-to-all-done = bf16[2,176,4096]{1,0,2:T(2,128)(2,1)} async-done(((bf16[2,176,4096]{1,0,2:T(2,128)(2,1)}), bf16[2,176,4096]{1,0,2:T(2,128)(2,1)}, u32[]{:S(2)}, u32[]{:S(2)}) %all-to-all-start) | async-done | bytes 2883616 | tf_op jit(solution)/shard_map/all_to_all | solution.py:176
  228.6 9.8 %fusion.66 = (bf16[1,176,4096]{1,0,2:T(2,128)(2,1)}, bf16[1,176,4096]{1,0,2:T(2,128)(2,1)}) fusion(bf16[2,176,4096]{1,0,2:T(2,128)(2,1)} %all-to-all-done), kind=kLoop, calls=%fused_computation.118 | loop fusion | bytes 5767168 | tf_op jit(solution)/shard_map/slice | solution.py:180
  238.3 9.6 %copy.42 = bf16[1,176,4096]{2,1,0:T(8,128)(2,1)} copy(bf16[1,176,4096]{1,0,2:T(2,128)(2,1)} %get-tuple-element.41) | data formatting | bytes 2883584 | tf_op jit(solution)/shard_map/slice | solution.py:180
  247.9 9.8 %copy.45 = bf16[1,176,4096]{2,1,0:T(8,128)(2,1)S(1)} copy(bf16[1,176,4096]{1,0,2:T(2,128)(2,1)} %get-tuple-element.42) | data formatting | bytes 2883584 | tf_op jit(solution)/shard_map/slice | solution.py:179
  257.7 3.7 %fusion = (f32[2,512]{1,0:T(2,128)S(1)}, f32[2,512,4096]{2,1,0:T(8,128)S(1)}) fusion(pred[4096]{0:T(1024)(128)(4,1)S(1)} %and.63, bf16[2,88,4096]{2,1,0:T(8,128)(2,1)S(1)} %bitcast.48, bf16[2,44,512]{2,1,0:T(8,128)(2,1)} %copy-done.8, bf16[2,44,512]{2,1,0:T(8,128)(2,1)S(1)} %get-tuple-element.45), kind=kOutput, calls=%fused_computation.2 | convolution fusion | flops 751139840 | bytes 18407424 | tf_op jit(solution)/shard_map/while/body/eval_jaxpr/hdq,hdk->hqk/dot_general | solution.py:29
  261.5 5.1 %fusion.1 = f32[2,512]{1,0:T(2,128)S(1)} fusion(f32[2,512,4096]{2,1,0:T(8,128)S(1)} %get-tuple-element.60, f32[2,512]{1,0:T(2,128)S(1)} %get-tuple-element.59, pred[4096]{0:T(1024)(128)(4,1)S(1)} %and.63), kind=kLoop, calls=%fused_computation.3 | loop fusion | flops 20970496 | bytes 16789504 | tf_op jit(solution)/shard_map/while/body/eval_jaxpr/reduce_sum | solution.py:34
  268.1 13.2 %fusion.29 = bf16[2,88,512]{2,1,0:T(8,128)(2,1)} fusion(f32[2,88,512]{2,1,0:T(8,128)S(1)} %fusion.20, bf16[2,88,4096]{2,1,0:T(8,128)(2,1)S(1)} %bitcast.51, f32[2,512,4096]{2,1,0:T(8,128)S(1)} %get-tuple-element.60, f32[2,512]{1,0:T(2,128)S(1)} %get-tuple-element.59, pred[4096]{0:T(1024)(128)(4,1)S(1)} %and.63, f32[2,512]{1,0:T(2,128)S(1)} %get-tuple-element.28, ...), kind=kOutput, calls=%fused_computation.39 | convolution fusion | flops 4446322688 | bytes 18776064 | tf_op jit(solution)/shard_map/while/body/eval_jaxpr/hqk,hdk->hdq/dot_general | solution.py:35
  (78 shorter events, 19.1 us)
Async XLA Ops:
  7.2 21.5 %copy-start = (bf16[4,176,1408]{2,1,0:T(8,128)(2,1)S(1)}, bf16[4,176,1408]{2,1,0:T(8,128)(2,1)}, u32[]{:S(2)}) copy-start(bf16[4,176,1408]{2,1,0:T(8,128)(2,1)} %param.12) | copy-start | bytes 5947396
  7.2 62.0 %reduce-scatter.4.cloned.1.call-start = ((), (), s32[]{:S(2)}) async-start(), calls=%async_computation.6 | async-start | bytes 811008
  28.6 2.7 copy-start.11
  28.6 18.1 %copy-start.9 = (s32[64,128]{1,0:T(8,128)S(1)}, s32[64,128]{1,0:T(8,128)}, u32[]{:S(2)}) copy-start(s32[64,128]{1,0:T(8,128)} %param.18) | copy-start | bytes 98308
  32.2 38.2 %all-to-all-start.2 = ((s32[64,1,1]{2,1,0:T(1,128)}), s32[64,1,1]{2,1,0:T(1,128)S(1)}, u32[]{:S(2)}, u32[]{:S(2)}) async-start(s32[64,1,1]{2,1,0:T(1,128)} %copy.44), calls=%async_computation.2 | async-start | bytes 65536 | tf_op jit(solution)/shard_map/all_to_all | solution.py:104
  70.4 24.4 %all-to-all-start.1 = ((s32[1,1,128]{1,0,2:T(1,128)}), s32[1,1,128]{1,0,2:T(1,128)S(1)}, u32[]{:S(2)}, u32[]{:S(2)}) async-start(s32[1,1,128]{1,0,2:T(1,128)} %copy.43), calls=%async_computation.1 | async-start | bytes 131072 | tf_op jit(solution)/shard_map/all_to_all | solution.py:177
  94.8 27.1 %all-to-all-start.3 = ((bf16[64,4,176]{2,1,0:T(4,128)(2,1)}), bf16[64,4,176]{2,1,0:T(4,128)(2,1)S(1)}, u32[]{:S(2)}, u32[]{:S(2)}) async-start(bf16[64,4,176]{2,1,0:T(4,128)(2,1)} %reshape.266), calls=%async_computation.3 | async-start | bytes 262144 | tf_op jit(solution)/shard_map/all_to_all | solution.py:103
  121.9 13.5 %copy-start.10 = (bf16[176,512]{1,0:T(8,128)(2,1)S(1)}, bf16[176,512]{1,0:T(8,128)(2,1)}, u32[]{:S(2)}) copy-start(bf16[176,512]{1,0:T(8,128)(2,1)} %param.14) | copy-start | bytes 540676
  121.9 106.7 %all-to-all-start = ((bf16[2,176,4096]{1,0,2:T(2,128)(2,1)}), bf16[2,176,4096]{1,0,2:T(2,128)(2,1)}, u32[]{:S(2)}, u32[]{:S(2)}) async-start(bf16[2,176,4096]{1,0,2:T(2,128)(2,1)} %copy.41), calls=%async_computation | async-start | bytes 8388608 | tf_op jit(solution)/shard_map/all_to_all | solution.py:176
  132.7 58.0 %all-gather.2.cloned.1.call-start = ((), (), s32[]{:S(2)}) async-start(), calls=%async_computation.5 | async-start | bytes 1622016 | tf_op jit(solution)/shard_map/all_gather | solution.py:126
  150.5 44.8 %copy-start.4 = (pred[512,512]{0,1:T(8,128)(4,1)}, pred[512,512]{0,1:T(8,128)(4,1)S(1)}, u32[]{:S(2)}) copy-start(pred[512,512]{0,1:T(8,128)(4,1)S(1)} %iota_compare_fusion) | copy-start | bytes 786436
  193.6 1.0 copy-start.6
  194.6 2.6 copy-start.8
  195.2 1.4 copy-start.1
  261.4 5.2 %copy-start.2 = (f32[2,512,512]{1,2,0:T(8,128)S(1)}, f32[2,512,512]{1,2,0:T(8,128)}, u32[]{:S(2)}) copy-start(f32[2,512,512]{1,2,0:T(8,128)} %copy-done.1) | copy-start | bytes 6291460
  261.5 5.2 %copy-start.5 = (pred[512,512]{0,1:T(8,128)(4,1)S(1)}, pred[512,512]{0,1:T(8,128)(4,1)}, u32[]{:S(2)}) copy-start(pred[512,512]{0,1:T(8,128)(4,1)} %copy-done.4) | copy-start | bytes 786436
  261.5 5.2 %copy-start.7 = (bf16[1,176,512]{2,1,0:T(8,128)(2,1)S(1)}, bf16[1,176,512]{2,1,0:T(8,128)(2,1)}, u32[]{:S(2)}) copy-start(bf16[1,176,512]{2,1,0:T(8,128)(2,1)} %copy-done.6) | copy-start | bytes 540676
  266.6 1.5 copy-start.3
Sparse Core Ops, SparseCore 0:
  31.5 37.7 reduce-scatter.3
  149.8 40.8 all-gather.1
where the time goes:
time: 290 us; the launch traced here: 288 us
  waiting for transfers between devices  88.9 us (31%)
  local copies, waits for them, and re-layouts  57.9 us (20%)
  starting transfers between devices  44.4 us (15%)
  blocking collectives  33.4 us (12%)
  matrix products  28.9 us (10%)
  other arithmetic  19.6 us (7%)
  between operations  15.1 us (5%)
    all_gather x1, waiting for transfers between devices, shards(): lax.all_gather(normed, 'head', axis=0, tiled=True)  34.9 us
    all_to_all x1, waiting for transfers between devices, shards(): lax.all_to_all(outgoing, 'blk', split_axis=2, concat_axis=2, tiled=True)  31.4 us
    psum x1, blocking collectives, shards(): lax.psum((jnp.sum(floats, axis=1), jnp.sum(floats * floats, axis=1)), 'he...  20.3 us
    slice x2, local copies, waits for them, and re-layouts, shards(): cached_values = blocks_in[1].reshape(heads_here, HD, -1).astype(jnp.float32)  19.4 us
    dot_general x2, matrix products, softmax_part(): jnp.einsum('hqk,hdk->hdq', expo, values, precision=lax.Precision.HIGHEST)  14.7 us
    all_to_all x1, starting transfers between devices, shards(): lax.all_to_all(labels, 'blk', split_axis=2, concat_axis=2, tiled=True)  14.6 us
    all_to_all x1, starting transfers between devices, shards(): lax.all_to_all(starts, 'blk', split_axis=0, concat_axis=0, tiled=True)  14.5 us
    unnamed x3, waiting for transfers between devices  13.9 us
  transfers between devices with their start and end apart: 6, of which 4 were waited for; matrix products, arithmetic and copies ran while one was open for 17% of the time, Pallas kernels for 0%

commit v1 on v0

--- a/solution.py
+++ b/solution.py
@@ -8,6 +8,19 @@
 HD = 88
 BS = 32
 masked_score = -1e30
+
+
+def gather_around(array, axis, dim):
+    ways = lax.axis_size(axis)
+    up = [(d, (d + 1) % ways) for d in range(ways)]
+    down = [(d, (d - 1) % ways) for d in range(ways)]
+    earlier, later = ([array], [array])
+    for _ in range(ways // 2):
+        earlier.append(lax.ppermute(earlier[-1], axis, up))
+    for _ in range((ways - 1) // 2):
+        later.append(lax.ppermute(later[-1], axis, down))
+    line = jnp.concatenate([*earlier[::-1], *later[1:]], axis=dim)
+    return jnp.roll(line, (lax.axis_index(axis) - ways // 2) * array.shape[dim], axis=dim)
 
 
 def rotary_columns(values, places):
@@ -121,10 +134,7 @@
         jnp.bfloat16
     )
     projected = jnp.einsum(
-        "jod,dr->jor",
-        wqkv,
-        lax.all_gather(normed, "head", axis=0, tiled=True),
-        preferred_element_type=jnp.float32,
+        "jod,dr->jor", wqkv, gather_around(normed, "head", 0), preferred_element_type=jnp.float32
     )
     heads_here = local // HD
     projected = projected.reshape(3, heads_here, HD, rows_here)

time: 290 us -> 278 us (0.959)
  waiting for transfers between devices: 88.9 us -> 61.1 us
  starting transfers between devices: 44.4 us -> 59.2 us
  local copies, waits for them, and re-layouts: 57.9 us -> 61.9 us
    all_gather x1 -> x0, waiting for transfers between devices: 34.9 us -> none  [shards(): lax.all_gather(normed, 'head', axis=0, tiled=True)]
    ppermute x0 -> x7, starting transfers between devices: none -> 23.7 us  [the longest x3 14.3 us: gather_around(): later.append(lax.ppermute(later[-1], axis, down))]
    unnamed x3 -> x2, waiting for transfers between devices: 13.9 us -> 0.04 us
    all_to_all x1, waiting for transfers between devices: 0.01 us -> 10.3 us  [shards(): lax.all_to_all(outbound, 'blk', split_axis=0, concat_axis=0, tiled=True)]
    all_to_all x1, waiting for transfers between devices: 31.4 us -> 38.9 us  [shards(): lax.all_to_all(outgoing, 'blk', split_axis=2, concat_axis=2, tiled=True)]
    ppermute x0 -> x7, waiting for transfers between devices: none -> 5.8 us  [the longest x4 5.52 us: gather_around(): earlier.append(lax.ppermute(earlier[-1], axis, up))]
    all_to_all x1, starting transfers between devices: 10.8 us -> 5.43 us  [shards(): lax.all_to_all(outgoing, 'blk', split_axis=2, concat_axis=2, tiled=True)]
    unnamed x27 -> x40, local copies, waits for them, and re-layouts: 7.2 us -> 11.2 us
  transfers between devices with their start and end apart: 6 -> 12, of which waited for: 4 -> 7; matrix products, arithmetic and copies ran while one was open for 17% -> 19% of each run, Pallas kernels for 0% -> 0%
where the time goes in v1:
time: 278 us; the launch traced here: 276 us
  local copies, waits for them, and re-layouts  61.9 us (22%)
  waiting for transfers between devices  61.1 us (22%)
  starting transfers between devices  59.2 us (21%)
  blocking collectives  32 us (12%)
  matrix products  27.1 us (10%)
  other arithmetic  19.6 us (7%)
  between operations  15.3 us (6%)
    all_to_all x1, waiting for transfers between devices, shards(): lax.all_to_all(outgoing, 'blk', split_axis=2, concat_axis=2, tiled=True)  38.9 us
    psum x1, blocking collectives, shards(): lax.psum((jnp.sum(floats, axis=1), jnp.sum(floats * floats, axis=1)), 'he...  19.7 us
    slice x2, local copies, waits for them, and re-layouts, shards(): cached_values = blocks_in[1].reshape(heads_here, HD, -1).astype(jnp.float32)  19.4 us
    dot_general x2, matrix products, softmax_part(): jnp.einsum('hqk,hdk->hdq', expo, values, precision=lax.Precision.HIGHEST)  14.7 us
    ppermute x3, starting transfers between devices, gather_around(): later.append(lax.ppermute(later[-1], axis, down))  14.3 us
    all_to_all x1, starting transfers between devices, shards(): lax.all_to_all(labels, 'blk', split_axis=2, concat_axis=2, tiled=True)  13.8 us
    psum x1, blocking collectives, shards(): square_sums = lax.psum(jnp.sum(row_floats * row_floats, axis=0), 'head')  12.3 us
    all_to_all x1, starting transfers between devices, shards(): lax.all_to_all(starts, 'blk', split_axis=0, concat_axis=0, tiled=True)  11.6 us
  transfers between devices with their start and end apart: 12, of which 7 were waited for; matrix products, arithmetic and copies ran while one was open for 19% of the time, Pallas kernels for 0%

profile of v1, /device:TPU:1, one launch (start us, length us, event | category | flops | bytes accessed | tf_op | source)
XLA Modules:
  0.0 276.1 jit_solution(3973189513514807957)
XLA Ops:
  8.8 11.6 %all-to-all-start.2 = ((s32[64,1,1]{2,1,0:T(1,128)}), s32[64,1,1]{2,1,0:T(1,128)S(1)}, u32[]{:S(2)}, u32[]{:S(2)}) async-start(s32[64,1,1]{2,1,0:T(1,128)} %copy.44), calls=%async_computation.2 | async-start | bytes 65536 | tf_op jit(solution)/shard_map/all_to_all | solution.py:117
  21.5 19.7 %all-reduce = (f32[4,128]{1,0:T(4,128)S(1)}, f32[4,128]{1,0:T(4,128)S(1)}) all-reduce(f32[4,128]{1,0:T(4,128)S(1)} %get-tuple-element.23, f32[4,128]{1,0:T(4,128)S(1)} %get-tuple-element.22), channel_id=1, replica_groups=mesh['head'=8,'blk'=64] {'head'}, use_global_device_ids=true, to_apply=%region_11.12 | all-reduce | flops 1024 | bytes 8192 | tf_op jit(solution)/shard_map/psum | solution.py:80
  47.1 3.7 %copy.38 = bf16[2,176,2048]{1,2,0:T(8,128)(2,1)} copy(bf16[2,176,2048]{2,1,0:T(8,128)(2,1)} %param.17) | data formatting | bytes 2883584 | tf_op args[7]
  52.5 4.9 %convert_bitcast_fusion = bf16[2,176,128,32]{2,1,3,0:T(8,128)(2,1)} fusion(bf16[2,176,64,32]{1,3,2,0:T(8,128)(2,1)} %bitcast.47, s32[64]{0:T(128)S(1)} %get-tuple-element.61, pred[64]{0:T(512)(128)(4,1)S(1)} %get-tuple-element.24), kind=kOutput, calls=%fused_computation.13 | convolution fusion | flops 186007552 | bytes 4325696 | tf_op jit(solution)/shard_map/wo,cfob->cfwb/dot_general | solution.py:179
  58.1 7.7 %copy.40 = bf16[2,176,128,32]{1,3,2,0:T(8,128)(2,1)} copy(bf16[2,176,128,32]{2,1,3,0:T(8,128)(2,1)} %convert_bitcast_fusion) | data formatting | bytes 5767168 | tf_op jit(solution)/shard_map/convert_element_type | solution.py:181
  65.8 10.1 %copy.41 = bf16[2,176,4096]{1,0,2:T(2,128)(2,1)} copy(bf16[2,176,4096]{1,2,0:T(8,128)(2,1)} %bitcast.46) | data formatting | bytes 5767168 | tf_op jit(solution)/shard_map/reshape | solution.py:182
  76.7 13.8 %all-to-all-start.1 = ((s32[1,1,128]{1,0,2:T(1,128)}), s32[1,1,128]{1,0,2:T(1,128)S(1)}, u32[]{:S(2)}, u32[]{:S(2)}) async-start(s32[1,1,128]{1,0,2:T(1,128)} %copy.43), calls=%async_computation.1 | async-start | bytes 131072 | tf_op jit(solution)/shard_map/all_to_all | solution.py:187
  94.1 6.1 %all-to-all-done.1 = s32[1,1,128]{1,0,2:T(1,128)S(1)} async-done(((s32[1,1,128]{1,0,2:T(1,128)}), s32[1,1,128]{1,0,2:T(1,128)S(1)}, u32[]{:S(2)}, u32[]{:S(2)}) %all-to-all-start.1) | async-done | bytes 544 | tf_op jit(solution)/shard_map/all_to_all | solution.py:187
  100.2 4.6 %all-to-all-start.3 = ((bf16[64,4,176]{2,1,0:T(4,128)(2,1)}), bf16[64,4,176]{2,1,0:T(4,128)(2,1)S(1)}, u32[]{:S(2)}, u32[]{:S(2)}) async-start(bf16[64,4,176]{2,1,0:T(4,128)(2,1)} %reshape.266), calls=%async_computation.3 | async-start | bytes 262144 | tf_op jit(solution)/shard_map/all_to_all | solution.py:116
  105.1 10.3 %all-to-all-done.3 = bf16[64,4,176]{2,1,0:T(4,128)(2,1)S(1)} async-done(((bf16[64,4,176]{2,1,0:T(4,128)(2,1)}), bf16[64,4,176]{2,1,0:T(4,128)(2,1)S(1)}, u32[]{:S(2)}, u32[]{:S(2)}) %all-to-all-start.3) | async-done | bytes 90144 | tf_op jit(solution)/shard_map/all_to_all | solution.py:116
  115.3 5.4 %all-to-all-start = ((bf16[2,176,4096]{1,0,2:T(2,128)(2,1)}), bf16[2,176,4096]{1,0,2:T(2,128)(2,1)}, u32[]{:S(2)}, u32[]{:S(2)}) async-start(bf16[2,176,4096]{1,0,2:T(2,128)(2,1)} %copy.41), calls=%async_computation | async-start | bytes 8388608 | tf_op jit(solution)/shard_map/all_to_all | solution.py:186
  121.4 12.3 %psum.23 = f32[512]{0:T(512)S(1)} all-reduce(f32[512]{0:T(512)S(1)} %get-tuple-element.55), channel_id=1, replica_groups=mesh['head'=8,'blk'=64] {'head'}, use_global_device_ids=true, to_apply=%region_14.15 | all-reduce | flops 512 | bytes 4096 | tf_op jit(solution)/shard_map/psum | solution.py:131
  133.8 3.4 %collective-permute-start = (bf16[176,512]{1,0:T(8,128)(2,1)S(1)}, bf16[176,512]{1,0:T(8,128)(2,1)S(1)}, u32[]{:S(2)}, u32[]{:S(2)}) collective-permute-start(bf16[176,512]{1,0:T(8,128)(2,1)S(1)} %multiply_convert_fusion), channel_id=1, source_target_pairs={{0,64},{64,128},{128,192},{192,256},{256,320},{320,384},{384,448},... | collective-permute-start | bytes 540680 | tf_op jit(solution)/shard_map/ppermute | solution.py:19
  137.3 4.4 %collective-permute-done = bf16[176,512]{1,0:T(8,128)(2,1)S(1)} collective-permute-done((bf16[176,512]{1,0:T(8,128)(2,1)S(1)}, bf16[176,512]{1,0:T(8,128)(2,1)S(1)}, u32[]{:S(2)}, u32[]{:S(2)}) %collective-permute-start) | collective-permute-done | bytes 180256 | tf_op jit(solution)/shard_map/ppermute | solution.py:19
  144.2 4.3 %collective-permute-start.4 = (bf16[176,512]{1,0:T(8,128)(2,1)S(1)}, bf16[176,512]{1,0:T(8,128)(2,1)S(1)}, u32[]{:S(2)}, u32[]{:S(2)}) collective-permute-start(bf16[176,512]{1,0:T(8,128)(2,1)S(1)} %multiply_convert_fusion), channel_id=1, source_target_pairs={{0,448},{64,0},{128,64},{192,128},{256,192},{320,256},{384,320},{4... | collective-permute-start | bytes 540680 | tf_op jit(solution)/shard_map/ppermute | solution.py:21
  156.1 4.6 %collective-permute-start.5 = (bf16[176,512]{1,0:T(8,128)(2,1)S(1)}, bf16[176,512]{1,0:T(8,128)(2,1)S(1)}, u32[]{:S(2)}, u32[]{:S(2)}) collective-permute-start(bf16[176,512]{1,0:T(8,128)(2,1)S(1)} %collective-permute-done.4), channel_id=1, source_target_pairs={{0,448},{64,0},{128,64},{192,128},{256,192},{320,256},{384,320},{4... | collective-permute-start | bytes 540680 | tf_op jit(solution)/shard_map/ppermute | solution.py:21
  163.1 5.4 %collective-permute-start.6 = (bf16[176,512]{1,0:T(8,128)(2,1)S(1)}, bf16[176,512]{1,0:T(8,128)(2,1)S(1)}, u32[]{:S(2)}, u32[]{:S(2)}) collective-permute-start(bf16[176,512]{1,0:T(8,128)(2,1)S(1)} %collective-permute-done.5), channel_id=1, source_target_pairs={{0,448},{64,0},{128,64},{192,128},{256,192},{320,256},{384,320},{4... | collective-permute-start | bytes 540680 | tf_op jit(solution)/shard_map/ppermute | solution.py:21
  177.8 38.9 %all-to-all-done = bf16[2,176,4096]{1,0,2:T(2,128)(2,1)} async-done(((bf16[2,176,4096]{1,0,2:T(2,128)(2,1)}), bf16[2,176,4096]{1,0,2:T(2,128)(2,1)}, u32[]{:S(2)}, u32[]{:S(2)}) %all-to-all-start) | async-done | bytes 2883616 | tf_op jit(solution)/shard_map/all_to_all | solution.py:186
  216.7 9.8 %fusion.68 = (bf16[1,176,4096]{1,0,2:T(2,128)(2,1)}, bf16[1,176,4096]{1,0,2:T(2,128)(2,1)}) fusion(bf16[2,176,4096]{1,0,2:T(2,128)(2,1)} %all-to-all-done), kind=kLoop, calls=%fused_computation.136 | loop fusion | bytes 5767168 | tf_op jit(solution)/shard_map/slice | solution.py:190
  226.5 9.6 %copy.42 = bf16[1,176,4096]{2,1,0:T(8,128)(2,1)} copy(bf16[1,176,4096]{1,0,2:T(2,128)(2,1)} %get-tuple-element.41) | data formatting | bytes 2883584 | tf_op jit(solution)/shard_map/slice | solution.py:190
  236.1 9.8 %copy.45 = bf16[1,176,4096]{2,1,0:T(8,128)(2,1)S(1)} copy(bf16[1,176,4096]{1,0,2:T(2,128)(2,1)} %get-tuple-element.42) | data formatting | bytes 2883584 | tf_op jit(solution)/shard_map/slice | solution.py:189
  245.9 3.7 %fusion = (f32[2,512]{1,0:T(2,128)S(1)}, f32[2,512,4096]{2,1,0:T(8,128)S(1)}) fusion(pred[4096]{0:T(1024)(128)(4,1)S(1)} %and.68, bf16[2,88,4096]{2,1,0:T(8,128)(2,1)S(1)} %bitcast.48, bf16[2,44,512]{2,1,0:T(8,128)(2,1)} %copy-done.8, bf16[2,44,512]{2,1,0:T(8,128)(2,1)S(1)} %get-tuple-element.45), kind=kOutput, calls=%fused_computation.2 | convolution fusion | flops 751139840 | bytes 18407424 | tf_op jit(solution)/shard_map/while/body/eval_jaxpr/hdq,hdk->hqk/dot_general | solution.py:42
  249.6 4.9 %fusion.1 = f32[2,512]{1,0:T(2,128)S(1)} fusion(f32[2,512,4096]{2,1,0:T(8,128)S(1)} %get-tuple-element.60, f32[2,512]{1,0:T(2,128)S(1)} %get-tuple-element.59, pred[4096]{0:T(1024)(128)(4,1)S(1)} %and.68), kind=kLoop, calls=%fused_computation.3 | loop fusion | flops 20970496 | bytes 16789504 | tf_op jit(solution)/shard_map/while/body/eval_jaxpr/reduce_sum | solution.py:47
  256.1 13.2 %fusion.30 = bf16[2,88,512]{2,1,0:T(8,128)(2,1)} fusion(f32[2,88,512]{2,1,0:T(8,128)S(1)} %fusion.21, bf16[2,88,4096]{2,1,0:T(8,128)(2,1)S(1)} %bitcast.51, f32[2,512,4096]{2,1,0:T(8,128)S(1)} %get-tuple-element.60, f32[2,512]{1,0:T(2,128)S(1)} %get-tuple-element.59, pred[4096]{0:T(1024)(128)(4,1)S(1)} %and.68, f32[2,512]{1,0:T(2,128)S(1)} %get-tuple-element.28, ...), kind=kOutput, calls=%fused_computation.40 | convolution fusion | flops 4446322688 | bytes 18776064 | tf_op jit(solution)/shard_map/while/body/eval_jaxpr/hqk,hdk->hdq/dot_general | solution.py:48
  (105 shorter events, 38.7 us)
Async XLA Ops:
  7.2 34.0 %copy-start = (bf16[4,176,1408]{2,1,0:T(8,128)(2,1)S(1)}, bf16[4,176,1408]{2,1,0:T(8,128)(2,1)}, u32[]{:S(2)}) copy-start(bf16[4,176,1408]{2,1,0:T(8,128)(2,1)} %param.12) | copy-start | bytes 5947396
  7.2 37.4 %copy-start.9 = (s32[64,128]{1,0:T(8,128)S(1)}, s32[64,128]{1,0:T(8,128)}, u32[]{:S(2)}) copy-start(s32[64,128]{1,0:T(8,128)} %param.18) | copy-start | bytes 98308
  8.8 67.9 %all-to-all-start.2 = ((s32[64,1,1]{2,1,0:T(1,128)}), s32[64,1,1]{2,1,0:T(1,128)S(1)}, u32[]{:S(2)}, u32[]{:S(2)}) async-start(s32[64,1,1]{2,1,0:T(1,128)} %copy.44), calls=%async_computation.2 | async-start | bytes 65536 | tf_op jit(solution)/shard_map/all_to_all | solution.py:117
  20.4 71.5 %reduce-scatter.4.cloned.1.call-start = ((), (), s32[]{:S(2)}) async-start(), calls=%async_computation.5 | async-start | bytes 811008
  76.7 23.6 %all-to-all-start.1 = ((s32[1,1,128]{1,0,2:T(1,128)}), s32[1,1,128]{1,0,2:T(1,128)S(1)}, u32[]{:S(2)}, u32[]{:S(2)}) async-start(s32[1,1,128]{1,0,2:T(1,128)} %copy.43), calls=%async_computation.1 | async-start | bytes 131072 | tf_op jit(solution)/shard_map/all_to_all | solution.py:187
  100.2 15.1 %all-to-all-start.3 = ((bf16[64,4,176]{2,1,0:T(4,128)(2,1)}), bf16[64,4,176]{2,1,0:T(4,128)(2,1)S(1)}, u32[]{:S(2)}, u32[]{:S(2)}) async-start(bf16[64,4,176]{2,1,0:T(4,128)(2,1)} %reshape.266), calls=%async_computation.3 | async-start | bytes 262144 | tf_op jit(solution)/shard_map/all_to_all | solution.py:116
  105.1 16.0 %copy-start.11 = (bf16[176,512]{1,0:T(8,128)(2,1)S(1)}, bf16[176,512]{1,0:T(8,128)(2,1)}, u32[]{:S(2)}) copy-start(bf16[176,512]{1,0:T(8,128)(2,1)} %param.14) | copy-start | bytes 540676
  115.3 101.4 %all-to-all-start = ((bf16[2,176,4096]{1,0,2:T(2,128)(2,1)}), bf16[2,176,4096]{1,0,2:T(2,128)(2,1)}, u32[]{:S(2)}, u32[]{:S(2)}) async-start(bf16[2,176,4096]{1,0,2:T(2,128)(2,1)} %copy.41), calls=%async_computation | async-start | bytes 8388608 | tf_op jit(solution)/shard_map/all_to_all | solution.py:186
  133.8 7.8 %collective-permute-start = (bf16[176,512]{1,0:T(8,128)(2,1)S(1)}, bf16[176,512]{1,0:T(8,128)(2,1)S(1)}, u32[]{:S(2)}, u32[]{:S(2)}) collective-permute-start(bf16[176,512]{1,0:T(8,128)(2,1)S(1)} %multiply_convert_fusion), channel_id=1, source_target_pairs={{0,64},{64,128},{128,192},{192,256},{256,320},{320,384},{384,448},... | collective-permute-start | bytes 540680 | tf_op jit(solution)/shard_map/ppermute | solution.py:19
  137.2 38.6 %copy-start.4 = (pred[512,512]{0,1:T(8,128)(4,1)}, pred[512,512]{0,1:T(8,128)(4,1)S(1)}, u32[]{:S(2)}) copy-start(pred[512,512]{0,1:T(8,128)(4,1)S(1)} %iota_compare_fusion) | copy-start | bytes 786436
  141.6 7.8 %collective-permute-start.1 = (bf16[176,512]{1,0:T(8,128)(2,1)S(1)}, bf16[176,512]{1,0:T(8,128)(2,1)S(1)}, u32[]{:S(2)}, u32[]{:S(2)}) collective-permute-start(bf16[176,512]{1,0:T(8,128)(2,1)S(1)} %collective-permute-done), channel_id=1, source_target_pairs={{0,64},{64,128},{128,192},{192,256},{256,320},{320,384},{384,448},... | collective-permute-start | bytes 540680 | tf_op jit(solution)/shard_map/ppermute | solution.py:19
  144.2 11.9 %collective-permute-start.4 = (bf16[176,512]{1,0:T(8,128)(2,1)S(1)}, bf16[176,512]{1,0:T(8,128)(2,1)S(1)}, u32[]{:S(2)}, u32[]{:S(2)}) collective-permute-start(bf16[176,512]{1,0:T(8,128)(2,1)S(1)} %multiply_convert_fusion), channel_id=1, source_target_pairs={{0,448},{64,0},{128,64},{192,128},{256,192},{320,256},{384,320},{4... | collective-permute-start | bytes 540680 | tf_op jit(solution)/shard_map/ppermute | solution.py:21
  149.5 11.2 %collective-permute-start.2 = (bf16[176,512]{1,0:T(8,128)(2,1)S(1)}, bf16[176,512]{1,0:T(8,128)(2,1)}, u32[]{:S(2)}, u32[]{:S(2)}) collective-permute-start(bf16[176,512]{1,0:T(8,128)(2,1)S(1)} %collective-permute-done.1), channel_id=1, source_target_pairs={{0,64},{64,128},{128,192},{192,256},{256,320},{320,384},{384,448},... | collective-permute-start | bytes 540680 | tf_op jit(solution)/shard_map/ppermute | solution.py:19
  156.1 7.0 %collective-permute-start.5 = (bf16[176,512]{1,0:T(8,128)(2,1)S(1)}, bf16[176,512]{1,0:T(8,128)(2,1)S(1)}, u32[]{:S(2)}, u32[]{:S(2)}) collective-permute-start(bf16[176,512]{1,0:T(8,128)(2,1)S(1)} %collective-permute-done.4), channel_id=1, source_target_pairs={{0,448},{64,0},{128,64},{192,128},{256,192},{320,256},{384,320},{4... | collective-permute-start | bytes 540680 | tf_op jit(solution)/shard_map/ppermute | solution.py:21
  160.7 8.1 %collective-permute-start.3 = (bf16[176,512]{1,0:T(8,128)(2,1)}, bf16[176,512]{1,0:T(8,128)(2,1)}, u32[]{:S(2)}, u32[]{:S(2)}) collective-permute-start(bf16[176,512]{1,0:T(8,128)(2,1)} %collective-permute-done.2), channel_id=1, source_target_pairs={{0,64},{64,128},{128,192},{192,256},{256,320},{320,384},{384,448},... | collective-permute-start | bytes 540680 | tf_op jit(solution)/shard_map/ppermute | solution.py:19
  163.1 7.8 %collective-permute-start.6 = (bf16[176,512]{1,0:T(8,128)(2,1)S(1)}, bf16[176,512]{1,0:T(8,128)(2,1)S(1)}, u32[]{:S(2)}, u32[]{:S(2)}) collective-permute-start(bf16[176,512]{1,0:T(8,128)(2,1)S(1)} %collective-permute-done.5), channel_id=1, source_target_pairs={{0,448},{64,0},{128,64},{192,128},{256,192},{320,256},{384,320},{4... | collective-permute-start | bytes 540680 | tf_op jit(solution)/shard_map/ppermute | solution.py:21
  169.7 3.4 %copy-start.10 = (bf16[3,176,1408]{2,1,0:T(8,128)(2,1)S(1)}, bf16[3,176,1408]{2,1,0:T(8,128)(2,1)}, u32[]{:S(2)}) copy-start(bf16[3,176,1408]{2,1,0:T(8,128)(2,1)} %param.16) | copy-start | bytes 4460548
  174.2 1.0 copy-start.6
  175.2 51.3 %copy-start.8 = (bf16[2,44,512]{2,1,0:T(8,128)(2,1)}, bf16[2,44,512]{2,1,0:T(8,128)(2,1)S(1)}, u32[]{:S(2)}) copy-start(bf16[2,44,512]{2,1,0:T(8,128)(2,1)S(1)} %get-tuple-element.46) | copy-start | bytes 270340
  175.8 1.4 copy-start.1
  249.6 4.9 %copy-start.2 = (f32[2,512,512]{1,2,0:T(8,128)S(1)}, f32[2,512,512]{1,2,0:T(8,128)}, u32[]{:S(2)}) copy-start(f32[2,512,512]{1,2,0:T(8,128)} %copy-done.1) | copy-start | bytes 6291460
  249.6 4.9 %copy-start.5 = (pred[512,512]{0,1:T(8,128)(4,1)S(1)}, pred[512,512]{0,1:T(8,128)(4,1)}, u32[]{:S(2)}) copy-start(pred[512,512]{0,1:T(8,128)(4,1)} %copy-done.4) | copy-start | bytes 786436
  249.6 4.9 %copy-start.7 = (bf16[1,176,512]{2,1,0:T(8,128)(2,1)S(1)}, bf16[1,176,512]{2,1,0:T(8,128)(2,1)}, u32[]{:S(2)}) copy-start(bf16[1,176,512]{2,1,0:T(8,128)(2,1)} %copy-done.6) | copy-start | bytes 540676
  254.5 1.5 copy-start.3
Sparse Core Ops, SparseCore 0:
  44.1 36.3 reduce-scatter.3
